TPU v7x, 32 devices: a whole 2x2x4 slice. The times are simulated.
32 devices in a mesh: head: 4 (over x, core), ctx: 8 (over z, y).
Axes of the slice: x: 2, y: 2, z: 4, core: 2. Of those that a mesh axis runs over, the one named last changes fastest.
Arguments:
- queries: bfloat16 [4096, 512], P(('ctx', 'head')), may hold values from -24 to 24
- key_vectors: bfloat16 [4096, 512], P(('ctx', 'head')), may hold values from -24 to 24
- value_vectors: bfloat16 [4096, 512], P(('ctx', 'head')), may hold values from -24 to 24
- window: int32 [4], P('head'), may hold values from 48 to 384, as said below
- block_order: int32 [32], replicated, may hold values from 0 to 31, as said below
Outputs:
- grad_queries: float32 [4096, 512], P('ctx', 'head')
- grad_keys: float32 [4096, 512], P('ctx', 'head')
- grad_values: float32 [4096, 512], P('ctx', 'head')
Inputs may be any that keep to these rules, and one draw needn't show every extreme that they name: `window`: some head has the reach 384 exactly. `block_order`: a permutation of 0 to 31 that maps each aligned group of 4 entries onto itself: entry g and its value lie in the same group.
All inputs are finite; a program needn't handle non-finite values.
Results may differ from a plain program's by a relative error of at most 0.039.
Values may be sent and summed in bfloat16 or wider, within the bound.
A program may use at most 64 MiB of HBM per device.

v0:
```python
import functools

import jax
import jax.numpy as jnp
from jax import lax
from jax.experimental import pallas as pl
from jax.experimental.pallas import tpu as pltpu
from jax.sharding import PartitionSpec as P

DH = 128
BLK = 128
RMAX = 384
HALO = RMAX // BLK
LOG2E = 1.4426950408889634
MESH = pl.DeviceIdType.MESH
NEG = -1e30


def dot_nt(a, b):
    return lax.dot_general(a, b, (((1,), (1,)), ((), ())), preferred_element_type=jnp.float32)


def dot_nn(a, b):
    return lax.dot_general(a, b, (((1,), (0,)), ((), ())), preferred_element_type=jnp.float32)


def dot_tn(a, b):
    return lax.dot_general(a, b, (((0,), (0,)), ((), ())), preferred_element_type=jnp.float32)


def grid_of(n):
    ny = 1
    while ny * ny * 8 <= n and n % (ny * 2) == 0:
        ny *= 2
    return n // ny, ny


def place_of(index, n):
    nz, ny = grid_of(n)
    z, y = index // ny, index % ny
    odd = y % 2
    return y * nz + z * (1 - odd) + (nz - 1 - z) * odd


def index_at(place, n):
    nz, ny = grid_of(n)
    y, r = place // nz, place % nz
    odd = y % 2
    z = r * (1 - odd) + (nz - 1 - r) * odd
    return z * ny + y


def kernel(
    n, g,
    window_ref, order_ref, q_ref, k_ref, v_ref,
    gq_s, gk_s, gv_s,
    qx, kv, qs, kpos, vpos, top_s, sum_s, acc_s, reach_s,
    a_send, a_recv, q_send, q_recv, r_send, r_recv, w_sem,
):
    c = lax.axis_index("ctx")
    h = lax.axis_index("head")
    part = q_ref.shape[0]
    rows = part * g
    nb = rows // BLK
    pieces = min(g, 4)
    per = g // pieces
    prow = rows // pieces
    half = n // 2
    nq = nb + 2 * HALO
    nk = nb + 4 * HALO
    scale = DH ** -0.5
    scale2 = scale * LOG2E
    place = place_of(c, n)
    right = index_at((place + 1) % n, n)
    left = index_at((place + n - 1) % n, n)
    ways = (right, left)

    barrier = pltpu.get_barrier_semaphore()
    for d in range(1, g):
        pl.semaphore_signal(barrier, inc=1, device_id={"head": (h + d) % g}, device_id_type=MESH)
    for way in ways:
        pl.semaphore_signal(barrier, inc=1, device_id={"ctx": way}, device_id_type=MESH)

    @pl.when(c > 0)
    def _():
        pl.semaphore_signal(barrier, inc=1, device_id={"ctx": c - 1}, device_id_type=MESH)

    @pl.when(c < n - 1)
    def _():
        pl.semaphore_signal(barrier, inc=1, device_id={"ctx": c + 1}, device_id_type=MESH)

    reach_copy = pltpu.make_async_copy(window_ref, reach_s, w_sem.at[0])
    reach_copy.start()
    pl.semaphore_wait(barrier, g + 1 + jnp.minimum(c, 1) + jnp.minimum(n - 1 - c, 1))

    mine = pl.ds(pl.multiple_of(h * part, part), part)

    def spread(d, which):
        peer = (h + d) % g
        cols = pl.ds(pl.multiple_of(peer * DH, DH), DH)
        src = (k_ref, v_ref, q_ref)[which].at[:, cols]
        dst = qx.at[1, mine] if which == 2 else kv.at[c, which, mine]
        if d == 0:
            return pltpu.make_async_copy(src, dst, a_recv.at[which, 0])
        return pltpu.make_async_remote_copy(
            src_ref=src, dst_ref=dst, send_sem=a_send.at[which, d], recv_sem=a_recv.at[which, d],
            device_id={"head": peer}, device_id_type=MESH,
        )

    for d in range(g):
        spread(d, 0).start()
        spread(d, 1).start()
    for d in range(g):
        spread(d, 2).start()

    def arrived(d, which):
        if d == 0:
            spread(0, which).wait()
        else:
            spread(d, which).wait_recv()

    def piece_of(d):
        return (h // per + pieces - d) % pieces

    def hop(way, step, d):
        sign = 1 if way == 0 else n - 1
        owner = index_at((place + step * (n - sign)) % n, n)
        span = pl.ds(pl.multiple_of(piece_of(d) * prow, prow), prow)
        ref = kv.at[owner, :, span]
        return pltpu.make_async_remote_copy(
            src_ref=ref, dst_ref=ref, send_sem=r_send.at[way, step, d], recv_sem=r_recv.at[way, step, d],
            device_id={"ctx": ways[way]}, device_id_type=MESH,
        )

    def landed(way, step, d):
        hop(way, step, d).wait_recv()

    if per == 1:
        for d in range(pieces):
            arrived(d, 0)
            arrived(d, 1)
            for way in range(2):
                hop(way, 0, d).start()
    else:
        for d in range(g):
            arrived(d, 0)
            arrived(d, 1)
        for d in range(pieces):
            for way in range(2):
                hop(way, 0, d).start()
    for d in range(g):
        arrived(d, 2)

    def beside(up):
        return pltpu.make_async_remote_copy(
            src_ref=qx.at[1], dst_ref=qx.at[0 if up else 2],
            send_sem=q_send.at[1 if up else 0], recv_sem=q_recv.at[1 if up else 0],
            device_id={"ctx": (c + 1) if up else (c - 1)}, device_id_type=MESH,
        )

    @pl.when(c > 0)
    def _():
        beside(False).start()

    @pl.when(c < n - 1)
    def _():
        beside(True).start()

    def sends_at(way, d, step_last):
        return (not step_last) or ((d < pieces // 2) == (way == 0))

    def forward(step, step_last, d):
        for way in range(2):
            landed(way, step - 1, d)
            if sends_at(way, d, step_last):
                hop(way, step, d).start()

    for d in range(pieces):
        forward(1, half == 2, d)

    @pl.when(c > 0)
    def _():
        beside(True).wait_recv()

    @pl.when(c < n - 1)
    def _():
        beside(False).wait_recv()

    def picked(blocks, group, p):
        found = blocks(0)
        for i in range(1, nb):
            found = jnp.where(order_ref[group * nb + i] == group * nb + p, blocks(i), found)
        return found

    groups = {}
    for off in range(-2, 3):
        groups[off] = jnp.clip(c + off, 0, n - 1)
    for m in range(nq):
        off, p = (m - HALO) // nb, (m - HALO) % nb
        slot = 1 + groups[off] - c
        qs[pl.ds(m * BLK, BLK), :] = picked(lambda i: qx[slot, pl.ds(i * BLK, BLK), :], groups[off], p)

    top_s[...] = jnp.full(top_s.shape, NEG, jnp.float32)
    sum_s[...] = jnp.zeros(sum_s.shape, jnp.float32)
    acc_s[...] = jnp.zeros(acc_s.shape, jnp.float32)

    qrow = nq * BLK // pieces

    def fold(u, owners, size=qrow):
        span = pl.ds(u * size, size)
        q = qs[span, :]
        scores = [dot_nt(q, kv[o, 0]) * scale2 for o in owners]
        top_old = top_s[span, :]
        highest = scores[0]
        for s in scores[1:]:
            highest = jnp.maximum(highest, s)
        top = jnp.maximum(top_old, jnp.max(highest, axis=1, keepdims=True))
        shrink = jnp.exp2(top_old - top)
        total = sum_s[span, :] * shrink
        acc = acc_s[span, :] * shrink
        for s, o in zip(scores, owners):
            e = jnp.exp2(s - top[:, :1])
            for i in range(rows // 128):
                total = total + e[:, i * 128 : (i + 1) * 128]
            acc = acc + dot_nn(e.astype(jnp.bfloat16), kv[o, 1])
        top_s[span, :] = top
        sum_s[span, :] = total
        acc_s[span, :] = acc

    def pair_at(step):
        return [index_at((place + n - step) % n, n), index_at((place + step) % n, n)]

    for u in range(pieces):
        fold(u, [c])

    def middle(step, carry):
        for d in range(pieces):
            forward(step, False, d)
            fold(d, pair_at(step - 1))
        return carry

    if half > 2:
        lax.fori_loop(2, half - 1, middle, 0)
        for d in range(pieces):
            forward(half - 1, True, d)
            fold(d, pair_at(half - 2))
    for d in range(pieces):
        fold(d, pair_at(half - 1))
    for d in range(pieces):
        for way in range(2):
            if sends_at(way, d, True):
                landed(way, half - 1, d)
    reach_copy.wait()
    for k in range(nk):
        off, p = (k - 2 * HALO) // nb, (k - 2 * HALO) % nb
        group = groups[off]
        for which, to in ((0, kpos), (1, vpos)):
            to[pl.ds(k * BLK, BLK), :] = picked(
                lambda i: kv[group, which, pl.ds(i * BLK, BLK), :], group, p
            )

    reach = reach_s[0]
    unit = 2
    units = nq // unit
    wide = 2 * HALO + unit
    usize = unit * BLK
    last = [index_at((place + half) % n, n)]
    gk_s[...] = jnp.zeros(gk_s.shape, jnp.float32)
    gv_s[...] = jnp.zeros(gv_s.shape, jnp.float32)
    held = {}

    def student_of(u):
        m = u * unit
        keys = pl.ds(m * BLK, wide * BLK)
        s = dot_nt(qs[pl.ds(m * BLK, usize), :], kpos[keys, :]) * scale2
        first = (c * nb + m - 2 * HALO) * BLK
        i = lax.broadcasted_iota(jnp.int32, (usize, 1), 0)
        j = lax.broadcasted_iota(jnp.int32, (usize, wide * BLK), 1)
        position = i + (first + HALO * BLK)
        i = i + HALO * BLK
        present = jnp.logical_and(position >= 0, position < n * rows)
        low = jnp.maximum(i - reach, -first)
        high = jnp.minimum(i + reach, n * rows - 1 - first)
        s = jnp.where(jnp.logical_and(j >= low, j <= high), s, NEG)
        top = jnp.max(s, axis=1, keepdims=True)
        e = jnp.exp2(s - top)
        inverse = jnp.where(present, 1.0 / jnp.sum(e, axis=1, keepdims=True), 0.0)
        prob = e * inverse
        prob_b = prob.astype(jnp.bfloat16)
        held[u] = (prob, prob_b, dot_nn(prob_b, vpos[keys, :]))

    def back_of(u):
        prob, prob_b, student = held.pop(u)
        m = u * unit
        span = pl.ds(m * BLK, usize)
        teacher = acc_s[span, :] * (1.0 / jnp.sum(sum_s[span, :], axis=1, keepdims=True))
        mismatch = student - teacher
        mismatch_b = mismatch.astype(jnp.bfloat16)
        delta = jnp.sum(mismatch * student, axis=1, keepdims=True)
        k0 = max(m, 2 * HALO)
        k1 = min(m + wide, 2 * HALO + nb)
        a0, a1 = (k0 - m) * BLK, (k1 - m) * BLK
        own = m + unit > HALO and m < HALO + nb
        if own:
            keys = pl.ds(m * BLK, wide * BLK)
            dprob = dot_nt(mismatch_b, vpos[keys, :])
            dscore = (prob * (dprob - delta)).astype(jnp.bfloat16)
            r0 = max(HALO - m, 0) * BLK
            r1 = min(HALO + nb - m, unit) * BLK
            gq_s[pl.ds((m - HALO) * BLK + r0, r1 - r0), :] = dot_nn(dscore[r0:r1], kpos[keys, :])
            dscore = dscore[:, a0:a1]
        else:
            dprob = dot_nt(mismatch_b, vpos[pl.ds(k0 * BLK, a1 - a0), :])
            dscore = (prob[:, a0:a1] * (dprob - delta)).astype(jnp.bfloat16)
        out = pl.ds((k0 - 2 * HALO) * BLK, a1 - a0)
        gk_s[out, :] += dot_tn(dscore, qs[span, :])
        gv_s[out, :] += dot_tn(prob_b[:, a0:a1], mismatch_b)

    for u in range(units + 1):
        if u < units:
            fold(u, last, usize)
            student_of(u)
        if u > 0:
            back_of(u - 1)

    for which in range(3):
        for d in range(1, g):
            spread(d, which).wait_send()

    @pl.when(c > 0)
    def _():
        beside(False).wait_send()

    @pl.when(c < n - 1)
    def _():
        beside(True).wait_send()

    def drain(step, carry):
        for d in range(pieces):
            for way in range(2):
                hop(way, step, d).wait_send()
        return carry

    lax.fori_loop(0, half - 1, drain, 0)
    for d in range(pieces):
        for way in range(2):
            if sends_at(way, d, True):
                hop(way, half - 1, d).wait_send()


def finish(order_ref, gq_s, gk_s, gv_s, gq_ref, gk_ref, gv_ref):
    nb = gq_ref.shape[0] // BLK
    c = lax.axis_index("ctx")
    scale = DH ** -0.5
    for b in range(nb):
        at = pl.ds(pl.multiple_of((order_ref[c * nb + b] - c * nb) * BLK, BLK), BLK)
        to = pl.ds(b * BLK, BLK)
        gq_ref[to, :] = gq_s[at, :] * scale
        gk_ref[to, :] = gk_s[at, :] * scale
        gv_ref[to, :] = gv_s[at, :]


def solution(mesh):
    n, g = mesh.shape["ctx"], mesh.shape["head"]

    def body(queries, key_vectors, value_vectors, window, block_order):
        part, width = queries.shape
        rows = part * g
        assert width == g * DH and rows % BLK == 0 and n >= 4 and n % 2 == 0
        nb = rows // BLK
        pieces = min(g, 4)
        half = n // 2
        tall_q = (nb + 2 * HALO) * BLK
        tall_k = (nb + 4 * HALO) * BLK
        out = jax.ShapeDtypeStruct((rows, DH), jnp.float32)
        vmem = pl.BlockSpec(memory_space=pltpu.VMEM)
        smem = pl.BlockSpec(memory_space=pltpu.SMEM)
        hbm = pl.BlockSpec(memory_space=pltpu.HBM)
        grads = pl.pallas_call(
            functools.partial(kernel, n, g),
            out_shape=(out, out, out),
            in_specs=[hbm, smem, hbm, hbm, hbm],
            out_specs=(vmem, vmem, vmem),
            scratch_shapes=[
                pltpu.VMEM((3, rows, DH), jnp.bfloat16),
                pltpu.VMEM((n, 2, rows, DH), jnp.bfloat16),
                pltpu.VMEM((tall_q, DH), jnp.bfloat16),
                pltpu.VMEM((tall_k, DH), jnp.bfloat16),
                pltpu.VMEM((tall_k, DH), jnp.bfloat16),
                pltpu.VMEM((tall_q, DH), jnp.float32),
                pltpu.VMEM((tall_q, DH), jnp.float32),
                pltpu.VMEM((tall_q, DH), jnp.float32),
                pltpu.SMEM((1,), jnp.int32),
                pltpu.SemaphoreType.DMA((3, g)),
                pltpu.SemaphoreType.DMA((3, g)),
                pltpu.SemaphoreType.DMA((2,)),
                pltpu.SemaphoreType.DMA((2,)),
                pltpu.SemaphoreType.DMA((2, half, pieces)),
                pltpu.SemaphoreType.DMA((2, half, pieces)),
                pltpu.SemaphoreType.DMA((1,)),
            ],
            compiler_params=pltpu.CompilerParams(collective_id=0, has_side_effects=True),
        )(window, block_order, queries, key_vectors, value_vectors)
        return pl.pallas_call(
            finish,
            out_shape=(out, out, out),
            in_specs=[smem, vmem, vmem, vmem],
            out_specs=(vmem, vmem, vmem),
        )(block_order, *grads)

    in_specs = (
        P(("ctx", "head"), None),
        P(("ctx", "head"), None),
        P(("ctx", "head"), None),
        P("head"),
        P(),
    )
    out_specs = (P("ctx", "head"), P("ctx", "head"), P("ctx", "head"))
    return jax.shard_map(body, mesh=mesh, in_specs=in_specs, out_specs=out_specs, check_vma=False)
```

profile of v0, /device:TPU:18, one launch (start us, length us, event | category | flops | bytes accessed | tf_op | source)
XLA Modules:
  0.0 46.1 jit_solution(18432643864627286184)
XLA Ops:
  1.3 42.8 %shard_map.76 = (f32[512,128]{1,0:T(8,128)}, f32[512,128]{1,0:T(8,128)}, f32[512,128]{1,0:T(8,128)}) custom-call(s32[1]{0:T(128)S(6)} %copy.8.window_ref, s32[32]{0:T(128)} %order_ref.3, bf16[128,512]{1,0:T(8,128)(2,1)} %q_ref.1, bf16[128,512]{1,0:T(8,128)(2,1)} %k_ref.1, bf16[128,512]{1,0:T(8,128)(2,1)} %v_ref.1), custom_call_target="tpu_custom_call" | custom-call | tf_op jit(solution)/shard_map/pallas_call | solution.py:379
  44.1 2.1 %shard_map.77 = (f32[512,128]{1,0:T(8,128)}, f32[512,128]{1,0:T(8,128)}, f32[512,128]{1,0:T(8,128)}) custom-call(s32[32]{0:T(128)} %order_ref.3, f32[512,128]{1,0:T(8,128)} %get-tuple-element.6.gq_s, f32[512,128]{1,0:T(8,128)} %get-tuple-element.7.gk_s, f32[512,128]{1,0:T(8,128)} %get-tuple-element.8.gv_s), custom_call_target="tpu_custom_call" | custom-call | tf_op jit(solution)/shard_map/pallas_call | solution.py:404
where the time goes:
time: 46.4 us; the launch traced here: 46.1 us
  Pallas kernels  44.9 us (97%)
  between operations  1.29 us (3%)
    pallas_call x1, Pallas kernels, body(): pl.pallas_call(functools.partial(kernel, n, g), out_shape=(out, out, out)...  42.8 us
    pallas_call x1, Pallas kernels, body(): pl.pallas_call(finish, out_shape=(out, out, out), in_specs=[smem, vmem, v...  2.07 us

commit v1 on v0

--- a/solution.py
+++ b/solution.py
@@ -70,6 +70,7 @@
     nk = nb + 4 * HALO
     scale = DH ** -0.5
     scale2 = scale * LOG2E
+    assert nb >= HALO
     place = place_of(c, n)
     right = index_at((place + 1) % n, n)
     left = index_at((place + n - 1) % n, n)
@@ -99,7 +100,7 @@
         peer = (h + d) % g
         cols = pl.ds(pl.multiple_of(peer * DH, DH), DH)
         src = (k_ref, v_ref, q_ref)[which].at[:, cols]
-        dst = qx.at[1, mine] if which == 2 else kv.at[c, which, mine]
+        dst = qx.at[mine] if which == 2 else kv.at[c, which, mine]
         if d == 0:
             return pltpu.make_async_copy(src, dst, a_recv.at[which, 0])
         return pltpu.make_async_remote_copy(
@@ -151,9 +152,24 @@
     for d in range(g):
         arrived(d, 2)
 
+    def picked(blocks, group, p):
+        found = blocks(0)
+        for i in range(1, nb):
+            found = jnp.where(order_ref[group * nb + i] == group * nb + p, blocks(i), found)
+        return found
+
+    edge = HALO * BLK
+    for p in range(nb):
+        qs[pl.ds(edge + p * BLK, BLK), :] = picked(lambda i: qx[pl.ds(i * BLK, BLK), :], c, p)
+
+    top_s[...] = jnp.full(top_s.shape, NEG, jnp.float32)
+    sum_s[...] = jnp.zeros(sum_s.shape, jnp.float32)
+    acc_s[...] = jnp.zeros(acc_s.shape, jnp.float32)
+
     def beside(up):
         return pltpu.make_async_remote_copy(
-            src_ref=qx.at[1], dst_ref=qx.at[0 if up else 2],
+            src_ref=qs.at[pl.ds(rows if up else edge, edge)],
+            dst_ref=qs.at[pl.ds(0 if up else edge + rows, edge)],
             send_sem=q_send.at[1 if up else 0], recv_sem=q_recv.at[1 if up else 0],
             device_id={"ctx": (c + 1) if up else (c - 1)}, device_id_type=MESH,
         )
@@ -162,9 +178,17 @@
     def _():
         beside(False).start()
 
+    @pl.when(c == 0)
+    def _():
+        qs[pl.ds(0, edge), :] = jnp.zeros((edge, DH), jnp.bfloat16)
+
     @pl.when(c < n - 1)
     def _():
         beside(True).start()
+
+    @pl.when(c == n - 1)
+    def _():
+        qs[pl.ds(edge + rows, edge), :] = jnp.zeros((edge, DH), jnp.bfloat16)
 
     def sends_at(way, d, step_last):
         return (not step_last) or ((d < pieces // 2) == (way == 0))
@@ -186,23 +210,9 @@
     def _():
         beside(False).wait_recv()
 
-    def picked(blocks, group, p):
-        found = blocks(0)
-        for i in range(1, nb):
-            found = jnp.where(order_ref[group * nb + i] == group * nb + p, blocks(i), found)
-        return found
-
     groups = {}
     for off in range(-2, 3):
         groups[off] = jnp.clip(c + off, 0, n - 1)
-    for m in range(nq):
-        off, p = (m - HALO) // nb, (m - HALO) % nb
-        slot = 1 + groups[off] - c
-        qs[pl.ds(m * BLK, BLK), :] = picked(lambda i: qx[slot, pl.ds(i * BLK, BLK), :], groups[off], p)
-
-    top_s[...] = jnp.full(top_s.shape, NEG, jnp.float32)
-    sum_s[...] = jnp.zeros(sum_s.shape, jnp.float32)
-    acc_s[...] = jnp.zeros(acc_s.shape, jnp.float32)
 
     qrow = nq * BLK // pieces
 
@@ -382,7 +392,7 @@
             in_specs=[hbm, smem, hbm, hbm, hbm],
             out_specs=(vmem, vmem, vmem),
             scratch_shapes=[
-                pltpu.VMEM((3, rows, DH), jnp.bfloat16),
+                pltpu.VMEM((rows, DH), jnp.bfloat16),
                 pltpu.VMEM((n, 2, rows, DH), jnp.bfloat16),
                 pltpu.VMEM((tall_q, DH), jnp.bfloat16),
                 pltpu.VMEM((tall_k, DH), jnp.bfloat16),

time: 46.4 us -> 45.1 us (0.972)
  Pallas kernels: 44.9 us -> 43.4 us
    pallas_call x1, Pallas kernels: 42.8 us -> 41.3 us  [body(): pl.pallas_call(functools.partial(kernel, n, g), out_shape=(out, out, out)...]
where the time goes in v1:
time: 45.1 us; the launch traced here: 44.6 us
  Pallas kernels  43.4 us (96%)
  between operations  1.29 us (3%)
    pallas_call x1, Pallas kernels, body(): pl.pallas_call(functools.partial(kernel, n, g), out_shape=(out, out, out)...  41.3 us
    pallas_call x1, Pallas kernels, body(): pl.pallas_call(finish, out_shape=(out, out, out), in_specs=[smem, vmem, v...  2.07 us

profile of v1, /device:TPU:18, one launch (start us, length us, event | category | flops | bytes accessed | tf_op | source)
XLA Modules:
  0.0 44.6 jit_solution(18077503319621684214)
XLA Ops:
  1.3 41.3 %shard_map.76 = (f32[512,128]{1,0:T(8,128)}, f32[512,128]{1,0:T(8,128)}, f32[512,128]{1,0:T(8,128)}) custom-call(s32[1]{0:T(128)S(6)} %copy.8.window_ref, s32[32]{0:T(128)} %order_ref.3, bf16[128,512]{1,0:T(8,128)(2,1)} %q_ref.1, bf16[128,512]{1,0:T(8,128)(2,1)} %k_ref.1, bf16[128,512]{1,0:T(8,128)(2,1)} %v_ref.1), custom_call_target="tpu_custom_call" | custom-call | tf_op jit(solution)/shard_map/pallas_call | solution.py:389
  42.6 2.1 %shard_map.77 = (f32[512,128]{1,0:T(8,128)}, f32[512,128]{1,0:T(8,128)}, f32[512,128]{1,0:T(8,128)}) custom-call(s32[32]{0:T(128)} %order_ref.3, f32[512,128]{1,0:T(8,128)} %get-tuple-element.6.gq_s, f32[512,128]{1,0:T(8,128)} %get-tuple-element.7.gk_s, f32[512,128]{1,0:T(8,128)} %get-tuple-element.8.gv_s), custom_call_target="tpu_custom_call" | custom-call | tf_op jit(solution)/shard_map/pallas_call | solution.py:414
